TPU v7x, 32 devices: a whole 2x2x4 slice. The times are simulated.
32 devices in a mesh: cell: 2 (over core), gene: 4 (over y, x), rank: 4 (over z).
Axes of the slice: x: 2, y: 2, z: 4, core: 2. Of those that a mesh axis runs over, the one named last changes fastest.
Arguments:
- blocks: bfloat16 [2, 16, 96, 256, 128], P('cell', ('gene', 'rank')), may hold values from -6 to 6
- block_pos: int32 [2, 16, 96], P('cell', ('gene', 'rank')), may hold values from 0 to 127, as said below
- block_count: int32 [2, 16], P('cell', ('gene', 'rank')), may hold values from 32 to 96, as said below
- test_right: bfloat16 [32768, 512], P(('gene', 'rank')), may hold values from -0.0625 to 0.0625
- test_left: bfloat16 [4096, 768], P('cell', 'rank'), may hold values from -0.1875 to 0.1875
- gene_sketch_old: float32 [768, 32768], P('cell', ('gene', 'rank')), may hold values from -4 to 4
Outputs:
- right_sketch: float32 [4096, 512], P(('cell', 'gene', 'rank'))
- gene_sketch: float32 [768, 32768], P('cell', ('gene', 'rank'))
- core: float32 [768, 512], P('cell')
Inputs may be any that keep to these rules, and one draw needn't show every extreme that they name: `block_pos`: position p names row block p // 16 and gene block p % 16 of the device's tile; the 96 positions of one device are distinct. `block_count`: some device has all 96 slots live in every draw; slots from the count on are not part of A.
All inputs are finite; a program needn't handle non-finite values.
Results may differ from a plain program's by a relative error of at most 0.0003.
Values may be sent and summed in bfloat16 or wider, within the bound.
A program may use at most 128 MiB of HBM per device.

v0:
```python
import jax
import jax.numpy as jnp
from jax import lax
from jax.sharding import PartitionSpec as P

GROUP = 16


def body(blocks, block_pos, block_count, test_right, test_left, gene_sketch_old):
    highest = lax.Precision.HIGHEST
    tiles = blocks[0, 0]
    positions = block_pos[0, 0]
    live_count = block_count[0, 0]
    slots, block_rows, block_cols = tiles.shape
    gene_blocks = test_right.shape[0] // block_cols
    right_width = test_right.shape[1]
    left_full = lax.all_gather(test_left, "rank", axis=1, tiled=True)
    row_blocks = left_full.shape[0] // block_rows
    left_width = left_full.shape[1]
    right_table = test_right.reshape(gene_blocks, block_cols, right_width)
    left_table = left_full.reshape(row_blocks, block_rows, left_width)
    offsets = jnp.arange(GROUP, dtype=jnp.int32)

    def visit(turn_index, carry):
        right_acc, gene_acc = carry
        first_slot = turn_index * GROUP
        group_tiles = lax.dynamic_slice_in_dim(tiles, first_slot, GROUP, 0)
        group_places = lax.dynamic_slice_in_dim(positions, first_slot, GROUP, 0)
        alive_mask = (first_slot + offsets < live_count).astype(jnp.float32)
        row_block = group_places // gene_blocks
        gene_block = group_places % gene_blocks
        right_rows = jnp.take(right_table, gene_block, axis=0)
        left_rows = jnp.take(left_table, row_block, axis=0)
        right_terms = (
            jnp.einsum("pik,pkr->pir", group_tiles, right_rows, preferred_element_type=jnp.float32)
            * alive_mask[:, None, None]
        )
        gene_terms = (
            jnp.einsum("pil,pik->lpk", left_rows, group_tiles, preferred_element_type=jnp.float32)
            * alive_mask[None, :, None]
        )
        right_acc = right_acc.at[row_block].add(right_terms)
        gene_acc = gene_acc.at[:, gene_block].add(gene_terms)
        return (right_acc, gene_acc)

    turn_count = (live_count + GROUP - 1) // GROUP
    initial = (
        jnp.zeros((row_blocks, block_rows, right_width), jnp.float32),
        jnp.zeros((left_width, gene_blocks, block_cols), jnp.float32),
    )
    right_part, gene_part = lax.fori_loop(0, turn_count, visit, initial)
    right_flat = right_part.reshape(row_blocks * block_rows, right_width)
    gene_flat = gene_part.reshape(left_width, gene_blocks * block_cols)
    right_half = lax.psum_scatter(right_flat, "gene", scatter_dimension=0, tiled=True)
    right_mine = lax.psum_scatter(right_half, "rank", scatter_dimension=0, tiled=True)
    gene_mine = lax.psum_scatter(gene_flat, "cell", scatter_dimension=0, tiled=True)
    gene_sketch = gene_sketch_old + gene_mine
    shard_index = lax.axis_index("gene") * lax.axis_size("rank") + lax.axis_index("rank")
    mine_rows = right_mine.shape[0]
    left_mine = lax.dynamic_slice_in_dim(left_full, shard_index * mine_rows, mine_rows, 0).astype(
        jnp.float32
    )
    core_part = lax.dot_general(left_mine, right_mine, (((0,), (0,)), ((), ())), precision=highest)
    core_total = lax.psum(core_part, ("cell", "gene", "rank"))
    share = left_width // lax.axis_size("cell")
    core = lax.dynamic_slice_in_dim(core_total, lax.axis_index("cell") * share, share, 0)
    return (right_mine, gene_sketch, core)


def solution(mesh):
    return jax.shard_map(
        body,
        mesh=mesh,
        in_specs=(
            P("cell", ("gene", "rank"), None, None, None),
            P("cell", ("gene", "rank"), None),
            P("cell", ("gene", "rank")),
            P(("gene", "rank"), None),
            P("cell", "rank"),
            P("cell", ("gene", "rank")),
        ),
        out_specs=(P(("cell", "gene", "rank"), None), P("cell", ("gene", "rank")), P("cell", None)),
        check_vma=False,
    )
```

profile of v0, /device:TPU:1, one launch (start us, length us, event | category | flops | bytes accessed | tf_op | source)
XLA Modules:
  0.0 695.8 jit_solution(15199658908383752672)
XLA Ops:
  8.6 66.3 %all-gather.2.cloned.1.call-done = bf16[2048,768]{0,1:T(8,128)(2,1)} async-done(((bf16[2048,192]{0,1:T(8,128)(2,1)}), bf16[2048,768]{0,1:T(8,128)(2,1)}) %all-gather.2.cloned.1.call-update) | async-done | bytes 3145744 | tf_op jit(solution)/shard_map/all_gather | solution.py:17
  84.0 305.6 %while.15 = (s32[]{:T(128)}, f32[8,256,512]{2,1,0:T(8,128)}, f32[768,16,128]{2,0,1:T(8,128)}, s32[]{:T(128)}, s32[96]{0:T(128)S(1)}, /*index=5*/bf16[96,256,128]...) while((s32[]{:T(128)}, f32[8,256,512]{2,1,0:T(8,128)}, ...), condition=%wide.region_3.4_spmd.clone, body=%wide.region_0.3_spmd.clone.sunk | while | flops 1353714176 | bytes 98575488 | solution.py:51
  88.3 7.2 %multiply_bitcast_fusion.2 = f32[16,768,128]{1,2,0:T(8,128)} fusion(f32[16]{0:T(128)S(1)} %get-tuple-element.245, bf16[16,256,768]{2,1,0:T(8,128)(2,1)} %gather_fusion.1, pred[16]{0:T(512)(128)(4,1)S(1)} %get-tuple-element.249, bf16[96,256,128]{2,1,0:T(8,128)(2,1)} %get-tuple-element.281, s32[]{:T(128)S(6)} %select_n.101), kind=kOutput, calls=%fused_computation.5.clone.1 | convolution fusion | flops 810024960 | bytes 13631572 | tf_op jit(solution)/shard_map/while/body/pil,pik->lpk/dot_general | solution.py:39
  95.5 6.5 copy.17
  102.0 15.0 %scatter_fusion.1 = f32[768,16,128]{2,0,1:T(8,128)} fusion(f32[768,16,128]{2,0,1:T(8,128)} %get-tuple-element.265, s32[16]{0:T(128)S(1)} %get-tuple-element.247, f32[16,768,128]{2,1,0:T(8,128)} %copy.17), kind=kCustom, calls=%fused_computation.3.clone.clone.1 | custom fusion | flops 1572864 | bytes 18874432 | tf_op jit(solution)/shard_map/while/body/scatter-add | solution.py:43
  127.1 18.1 %scatter_fusion = f32[8,256,512]{2,1,0:T(8,128)} fusion(f32[8,256,512]{2,1,0:T(8,128)} %get-tuple-element.264, s32[16]{0:T(128)S(1)} %get-tuple-element.244, f32[16,256,512]{2,1,0:T(8,128)} %broadcast_multiply_fusion.2), kind=kCustom, calls=%fused_computation.2.clone.clone.1 | custom fusion | flops 2097152 | bytes 25165888 | tf_op jit(solution)/shard_map/while/body/scatter-add | solution.py:42
  149.4 7.2 %multiply_bitcast_fusion.2 = f32[16,768,128]{1,2,0:T(8,128)} fusion(f32[16]{0:T(128)S(1)} %get-tuple-element.245, bf16[16,256,768]{2,1,0:T(8,128)(2,1)} %gather_fusion.1, pred[16]{0:T(512)(128)(4,1)S(1)} %get-tuple-element.249, bf16[96,256,128]{2,1,0:T(8,128)(2,1)} %get-tuple-element.281, s32[]{:T(128)S(6)} %select_n.101), kind=kOutput, calls=%fused_computation.5.clone.1 | convolution fusion | flops 810024960 | bytes 13631572 | tf_op jit(solution)/shard_map/while/body/pil,pik->lpk/dot_general | solution.py:39
  156.6 6.5 copy.17
  163.2 15.3 %scatter_fusion.1 = f32[768,16,128]{2,0,1:T(8,128)} fusion(f32[768,16,128]{2,0,1:T(8,128)} %get-tuple-element.265, s32[16]{0:T(128)S(1)} %get-tuple-element.247, f32[16,768,128]{2,1,0:T(8,128)} %copy.17), kind=kCustom, calls=%fused_computation.3.clone.clone.1 | custom fusion | flops 1572864 | bytes 18874432 | tf_op jit(solution)/shard_map/while/body/scatter-add | solution.py:43
  188.5 18.0 %scatter_fusion = f32[8,256,512]{2,1,0:T(8,128)} fusion(f32[8,256,512]{2,1,0:T(8,128)} %get-tuple-element.264, s32[16]{0:T(128)S(1)} %get-tuple-element.244, f32[16,256,512]{2,1,0:T(8,128)} %broadcast_multiply_fusion.2), kind=kCustom, calls=%fused_computation.2.clone.clone.1 | custom fusion | flops 2097152 | bytes 25165888 | tf_op jit(solution)/shard_map/while/body/scatter-add | solution.py:42
  210.8 7.2 %multiply_bitcast_fusion.2 = f32[16,768,128]{1,2,0:T(8,128)} fusion(f32[16]{0:T(128)S(1)} %get-tuple-element.245, bf16[16,256,768]{2,1,0:T(8,128)(2,1)} %gather_fusion.1, pred[16]{0:T(512)(128)(4,1)S(1)} %get-tuple-element.249, bf16[96,256,128]{2,1,0:T(8,128)(2,1)} %get-tuple-element.281, s32[]{:T(128)S(6)} %select_n.101), kind=kOutput, calls=%fused_computation.5.clone.1 | convolution fusion | flops 810024960 | bytes 13631572 | tf_op jit(solution)/shard_map/while/body/pil,pik->lpk/dot_general | solution.py:39
  218.0 6.5 copy.17
  224.6 14.9 %scatter_fusion.1 = f32[768,16,128]{2,0,1:T(8,128)} fusion(f32[768,16,128]{2,0,1:T(8,128)} %get-tuple-element.265, s32[16]{0:T(128)S(1)} %get-tuple-element.247, f32[16,768,128]{2,1,0:T(8,128)} %copy.17), kind=kCustom, calls=%fused_computation.3.clone.clone.1 | custom fusion | flops 1572864 | bytes 18874432 | tf_op jit(solution)/shard_map/while/body/scatter-add | solution.py:43
  249.6 18.0 %scatter_fusion = f32[8,256,512]{2,1,0:T(8,128)} fusion(f32[8,256,512]{2,1,0:T(8,128)} %get-tuple-element.264, s32[16]{0:T(128)S(1)} %get-tuple-element.244, f32[16,256,512]{2,1,0:T(8,128)} %broadcast_multiply_fusion.2), kind=kCustom, calls=%fused_computation.2.clone.clone.1 | custom fusion | flops 2097152 | bytes 25165888 | tf_op jit(solution)/shard_map/while/body/scatter-add | solution.py:42
  271.9 7.2 %multiply_bitcast_fusion.2 = f32[16,768,128]{1,2,0:T(8,128)} fusion(f32[16]{0:T(128)S(1)} %get-tuple-element.245, bf16[16,256,768]{2,1,0:T(8,128)(2,1)} %gather_fusion.1, pred[16]{0:T(512)(128)(4,1)S(1)} %get-tuple-element.249, bf16[96,256,128]{2,1,0:T(8,128)(2,1)} %get-tuple-element.281, s32[]{:T(128)S(6)} %select_n.101), kind=kOutput, calls=%fused_computation.5.clone.1 | convolution fusion | flops 810024960 | bytes 13631572 | tf_op jit(solution)/shard_map/while/body/pil,pik->lpk/dot_general | solution.py:39
  285.6 15.1 %scatter_fusion.1 = f32[768,16,128]{2,0,1:T(8,128)} fusion(f32[768,16,128]{2,0,1:T(8,128)} %get-tuple-element.265, s32[16]{0:T(128)S(1)} %get-tuple-element.247, f32[16,768,128]{2,1,0:T(8,128)} %copy.17), kind=kCustom, calls=%fused_computation.3.clone.clone.1 | custom fusion | flops 1572864 | bytes 18874432 | tf_op jit(solution)/shard_map/while/body/scatter-add | solution.py:43
  310.8 17.6 %scatter_fusion = f32[8,256,512]{2,1,0:T(8,128)} fusion(f32[8,256,512]{2,1,0:T(8,128)} %get-tuple-element.264, s32[16]{0:T(128)S(1)} %get-tuple-element.244, f32[16,256,512]{2,1,0:T(8,128)} %broadcast_multiply_fusion.2), kind=kCustom, calls=%fused_computation.2.clone.clone.1 | custom fusion | flops 2097152 | bytes 25165888 | tf_op jit(solution)/shard_map/while/body/scatter-add | solution.py:42
  332.7 7.2 %multiply_bitcast_fusion.2 = f32[16,768,128]{1,2,0:T(8,128)} fusion(f32[16]{0:T(128)S(1)} %get-tuple-element.245, bf16[16,256,768]{2,1,0:T(8,128)(2,1)} %gather_fusion.1, pred[16]{0:T(512)(128)(4,1)S(1)} %get-tuple-element.249, bf16[96,256,128]{2,1,0:T(8,128)(2,1)} %get-tuple-element.281, s32[]{:T(128)S(6)} %select_n.101), kind=kOutput, calls=%fused_computation.5.clone.1 | convolution fusion | flops 810024960 | bytes 13631572 | tf_op jit(solution)/shard_map/while/body/pil,pik->lpk/dot_general | solution.py:39
  346.4 15.1 %scatter_fusion.1 = f32[768,16,128]{2,0,1:T(8,128)} fusion(f32[768,16,128]{2,0,1:T(8,128)} %get-tuple-element.265, s32[16]{0:T(128)S(1)} %get-tuple-element.247, f32[16,768,128]{2,1,0:T(8,128)} %copy.17), kind=kCustom, calls=%fused_computation.3.clone.clone.1 | custom fusion | flops 1572864 | bytes 18874432 | tf_op jit(solution)/shard_map/while/body/scatter-add | solution.py:43
  371.7 18.0 %scatter_fusion = f32[8,256,512]{2,1,0:T(8,128)} fusion(f32[8,256,512]{2,1,0:T(8,128)} %get-tuple-element.264, s32[16]{0:T(128)S(1)} %get-tuple-element.244, f32[16,256,512]{2,1,0:T(8,128)} %broadcast_multiply_fusion.2), kind=kCustom, calls=%fused_computation.2.clone.clone.1 | custom fusion | flops 2097152 | bytes 25165888 | tf_op jit(solution)/shard_map/while/body/scatter-add | solution.py:42
  389.7 112.0 %reduce-scatter.4.cloned.1.call-done = f32[512,512]{1,0:T(8,128)} async-done(((f32[2048,512]{1,0:T(8,128)}), f32[512,512]{1,0:T(8,128)}) %reduce-scatter.4.cloned.1.call-update) | async-done | bytes 1048592 | tf_op jit(solution)/shard_map/reduce_scatter | solution.py:54
  501.8 29.9 %reduce-scatter.6.cloned.1.call-done = f32[128,512]{1,0:T(8,128)} async-done(((f32[512,512]{1,0:T(8,128)}), f32[128,512]{1,0:T(8,128)}) %reduce-scatter.6.cloned.1.call-update) | async-done | bytes 262160 | tf_op jit(solution)/shard_map/reduce_scatter | solution.py:55
  541.1 126.8 %all-reduce.2.cloned.1.call-done = f32[768,512]{1,0:T(8,128)} async-done(((f32[768,512]{1,0:T(8,128)}), f32[768,512]{1,0:T(8,128)}) %all-reduce.2.cloned.1.call-update) | async-done | bytes 1572880 | tf_op jit(solution)/shard_map/psum | solution.py:64
  670.0 15.3 %reduce-scatter.8.cloned.1.call-done = f32[384,2048]{1,0:T(8,128)} async-done(((f32[768,2048]{1,0:T(8,128)}), f32[384,2048]{1,0:T(8,128)}) %reduce-scatter.8.cloned.1.call-update) | async-done | bytes 3145744 | tf_op jit(solution)/shard_map/reduce_scatter | solution.py:56
  (58 shorter events, 110.3 us)
Async XLA Ops:
  7.2 67.8 %all-gather.2.cloned.1.call-start = ((), (), s32[]{:S(2)}) async-start(), calls=%async_computation.3 | async-start | bytes 3932160 | tf_op jit(solution)/shard_map/all_gather | solution.py:17
  7.9 493.9 %reduce-scatter.4.cloned.1.call-start = ((), (), s32[]{:S(2)}) async-start(), calls=%async_computation.4 | async-start | bytes 5242880 | tf_op jit(solution)/shard_map/reduce_scatter | solution.py:54
  78.1 5.9 copy-start.1
  389.7 142.1 %reduce-scatter.6.cloned.1.call-start = ((), (), s32[]{:S(2)}) async-start(), calls=%async_computation.5 | async-start | bytes 1310720 | tf_op jit(solution)/shard_map/reduce_scatter | solution.py:55
  501.8 166.1 %all-reduce.2.cloned.1.call-start = ((), (), s32[]{:S(2)}) async-start(), calls=%async_computation.7 | async-start | bytes 3145728 | tf_op jit(solution)/shard_map/psum | solution.py:64
  534.7 150.5 %reduce-scatter.8.cloned.1.call-start = ((), (), s32[]{:S(2)}) async-start(), calls=%async_computation.6 | async-start | bytes 9437184 | tf_op jit(solution)/shard_map/reduce_scatter | solution.py:56
  541.1 144.1 %copy-start = (f32[384,2048]{1,0:T(8,128)S(1)}, f32[384,2048]{1,0:T(8,128)}, u32[]{:S(2)}) copy-start(f32[384,2048]{1,0:T(8,128)} %param.13) | copy-start | bytes 9437188
Sparse Core Ops, SparseCore 0:
  9.5 65.3 all-gather.1
  389.8 111.9 reduce-scatter.3
  504.6 27.0 reduce-scatter.5
  537.4 130.4 all-reduce.1
  670.1 15.1 reduce-scatter.7
where the time goes:
time: 697 us; the launch traced here: 696 us
  waiting for transfers between devices  351 us (50%)
  other arithmetic  173 us (25%)
  local copies, waits for them, and re-layouts  85.8 us (12%)
  matrix products  71.3 us (10%)
  between operations  14.5 us (2%)
    psum x1, waiting for transfers between devices, body(): core_total = lax.psum(core_part, ('cell', 'gene', 'rank'))  127 us
    reduce_scatter x1, waiting for transfers between devices, body(): lax.psum_scatter(right_flat, 'gene', scatter_dimension=0, tiled=True)  112 us
    scatter-add x5, other arithmetic, visit(): right_acc = right_acc.at[row_block].add(right_terms)  89.7 us
    scatter-add x5, other arithmetic, visit(): gene_acc = gene_acc.at[:, gene_block].add(gene_terms)  75.5 us
    all_gather x1, waiting for transfers between devices, body(): left_full = lax.all_gather(test_left, 'rank', axis=1, tiled=True)  66.3 us
    dot_general x5, matrix products, visit(): jnp.einsum('pil,pik->lpk', left_rows, group_tiles, preferred_element_type...  35.9 us
    mul x5, local copies, waits for them, and re-layouts, visit(): jnp.einsum('pil,pik->lpk', left_rows, group_tiles, preferred_element_type...  32.7 us
    dot_general x5, matrix products, visit(): jnp.einsum('pik,pkr->pir', group_tiles, right_rows, preferred_element_typ...  32.4 us
  transfers between devices with their start and end apart: 5, of which 5 were waited for; matrix products, arithmetic and copies ran while one was open for 1% of the time, Pallas kernels for 0%

commit v1 on v0

--- a/solution.py
+++ b/solution.py
@@ -1,9 +1,19 @@
+import functools
 import jax
 import jax.numpy as jnp
 from jax import lax
 from jax.sharding import PartitionSpec as P
 
 GROUP = 16
+
+
+def check_sides(z, bus_axis, shard_axis):
+    for jj in (bus_axis, shard_axis):
+        z = lax.psum(z, jj)
+    return z
+
+
+handle_waves = functools.partial(check_sides, bus_axis="cell", shard_axis=("gene", "rank"))
 
 
 def body(blocks, block_pos, block_count, test_right, test_left, gene_sketch_old):
@@ -61,7 +71,7 @@
         jnp.float32
     )
     core_part = lax.dot_general(left_mine, right_mine, (((0,), (0,)), ((), ())), precision=highest)
-    core_total = lax.psum(core_part, ("cell", "gene", "rank"))
+    core_total = handle_waves(core_part)
     share = left_width // lax.axis_size("cell")
     core = lax.dynamic_slice_in_dim(core_total, lax.axis_index("cell") * share, share, 0)
     return (right_mine, gene_sketch, core)

time: 697 us -> 708 us (1.016)
  waiting for transfers between devices: 351 us -> 359 us
    psum x1 -> x2, waiting for transfers between devices: 127 us -> 133 us  [check_sides(): z = lax.psum(z, jj)]
  transfers between devices with their start and end apart: 5 -> 6, of which waited for: 5 -> 6; matrix products, arithmetic and copies ran while one was open for 1% -> 1% of each run, Pallas kernels for 0% -> 0%
where the time goes in v1:
time: 708 us; the launch traced here: 705 us
  waiting for transfers between devices  359 us (51%)
  other arithmetic  173 us (24%)
  local copies, waits for them, and re-layouts  85.9 us (12%)
  matrix products  71.3 us (10%)
  between operations  14.8 us (2%)
    psum x2, waiting for transfers between devices, check_sides(): z = lax.psum(z, jj)  133 us
    reduce_scatter x1, waiting for transfers between devices, body(): lax.psum_scatter(right_flat, 'gene', scatter_dimension=0, tiled=True)  112 us
    scatter-add x5, other arithmetic, visit(): right_acc = right_acc.at[row_block].add(right_terms)  89.7 us
    scatter-add x5, other arithmetic, visit(): gene_acc = gene_acc.at[:, gene_block].add(gene_terms)  75.5 us
    all_gather x1, waiting for transfers between devices, body(): left_full = lax.all_gather(test_left, 'rank', axis=1, tiled=True)  66.3 us
    dot_general x5, matrix products, visit(): jnp.einsum('pil,pik->lpk', left_rows, group_tiles, preferred_element_type...  35.9 us
    mul x5, local copies, waits for them, and re-layouts, visit(): jnp.einsum('pil,pik->lpk', left_rows, group_tiles, preferred_element_type...  32.7 us
    dot_general x5, matrix products, visit(): jnp.einsum('pik,pkr->pir', group_tiles, right_rows, preferred_element_typ...  32.4 us
  transfers between devices with their start and end apart: 6, of which 6 were waited for; matrix products, arithmetic and copies ran while one was open for 1% of the time, Pallas kernels for 0%

profile of v1, /device:TPU:1, one launch (start us, length us, event | category | flops | bytes accessed | tf_op | source)
XLA Modules:
  0.0 704.5 jit_solution(8445042487540783814)
XLA Ops:
  8.6 66.3 %all-gather.2.cloned.1.call-done = bf16[2048,768]{0,1:T(8,128)(2,1)} async-done(((bf16[2048,192]{0,1:T(8,128)(2,1)}), bf16[2048,768]{0,1:T(8,128)(2,1)}) %all-gather.2.cloned.1.call-update) | async-done | bytes 3145744 | tf_op jit(solution)/shard_map/all_gather | solution.py:27
  84.0 305.6 %while.15 = (s32[]{:T(128)}, f32[8,256,512]{2,1,0:T(8,128)}, f32[768,16,128]{2,0,1:T(8,128)}, s32[]{:T(128)}, s32[96]{0:T(128)S(1)}, /*index=5*/bf16[96,256,128]...) while((s32[]{:T(128)}, f32[8,256,512]{2,1,0:T(8,128)}, ...), condition=%wide.region_3.4_spmd.clone, body=%wide.region_0.3_spmd.clone.sunk | while | flops 1353714176 | bytes 98575488 | solution.py:61
  88.3 7.2 %multiply_bitcast_fusion.2 = f32[16,768,128]{1,2,0:T(8,128)} fusion(f32[16]{0:T(128)S(1)} %get-tuple-element.245, bf16[16,256,768]{2,1,0:T(8,128)(2,1)} %gather_fusion.1, pred[16]{0:T(512)(128)(4,1)S(1)} %get-tuple-element.249, bf16[96,256,128]{2,1,0:T(8,128)(2,1)} %get-tuple-element.281, s32[]{:T(128)S(6)} %select_n.101), kind=kOutput, calls=%fused_computation.5.clone.1 | convolution fusion | flops 810024960 | bytes 13631572 | tf_op jit(solution)/shard_map/while/body/pil,pik->lpk/dot_general | solution.py:49
  95.5 6.5 copy.17
  102.0 15.0 %scatter_fusion.1 = f32[768,16,128]{2,0,1:T(8,128)} fusion(f32[768,16,128]{2,0,1:T(8,128)} %get-tuple-element.265, s32[16]{0:T(128)S(1)} %get-tuple-element.247, f32[16,768,128]{2,1,0:T(8,128)} %copy.17), kind=kCustom, calls=%fused_computation.3.clone.clone.1 | custom fusion | flops 1572864 | bytes 18874432 | tf_op jit(solution)/shard_map/while/body/scatter-add | solution.py:53
  127.1 18.1 %scatter_fusion = f32[8,256,512]{2,1,0:T(8,128)} fusion(f32[8,256,512]{2,1,0:T(8,128)} %get-tuple-element.264, s32[16]{0:T(128)S(1)} %get-tuple-element.244, f32[16,256,512]{2,1,0:T(8,128)} %broadcast_multiply_fusion.2), kind=kCustom, calls=%fused_computation.2.clone.clone.1 | custom fusion | flops 2097152 | bytes 25165888 | tf_op jit(solution)/shard_map/while/body/scatter-add | solution.py:52
  149.4 7.2 %multiply_bitcast_fusion.2 = f32[16,768,128]{1,2,0:T(8,128)} fusion(f32[16]{0:T(128)S(1)} %get-tuple-element.245, bf16[16,256,768]{2,1,0:T(8,128)(2,1)} %gather_fusion.1, pred[16]{0:T(512)(128)(4,1)S(1)} %get-tuple-element.249, bf16[96,256,128]{2,1,0:T(8,128)(2,1)} %get-tuple-element.281, s32[]{:T(128)S(6)} %select_n.101), kind=kOutput, calls=%fused_computation.5.clone.1 | convolution fusion | flops 810024960 | bytes 13631572 | tf_op jit(solution)/shard_map/while/body/pil,pik->lpk/dot_general | solution.py:49
  156.6 6.5 copy.17
  163.2 15.3 %scatter_fusion.1 = f32[768,16,128]{2,0,1:T(8,128)} fusion(f32[768,16,128]{2,0,1:T(8,128)} %get-tuple-element.265, s32[16]{0:T(128)S(1)} %get-tuple-element.247, f32[16,768,128]{2,1,0:T(8,128)} %copy.17), kind=kCustom, calls=%fused_computation.3.clone.clone.1 | custom fusion | flops 1572864 | bytes 18874432 | tf_op jit(solution)/shard_map/while/body/scatter-add | solution.py:53
  188.5 18.0 %scatter_fusion = f32[8,256,512]{2,1,0:T(8,128)} fusion(f32[8,256,512]{2,1,0:T(8,128)} %get-tuple-element.264, s32[16]{0:T(128)S(1)} %get-tuple-element.244, f32[16,256,512]{2,1,0:T(8,128)} %broadcast_multiply_fusion.2), kind=kCustom, calls=%fused_computation.2.clone.clone.1 | custom fusion | flops 2097152 | bytes 25165888 | tf_op jit(solution)/shard_map/while/body/scatter-add | solution.py:52
  210.8 7.2 %multiply_bitcast_fusion.2 = f32[16,768,128]{1,2,0:T(8,128)} fusion(f32[16]{0:T(128)S(1)} %get-tuple-element.245, bf16[16,256,768]{2,1,0:T(8,128)(2,1)} %gather_fusion.1, pred[16]{0:T(512)(128)(4,1)S(1)} %get-tuple-element.249, bf16[96,256,128]{2,1,0:T(8,128)(2,1)} %get-tuple-element.281, s32[]{:T(128)S(6)} %select_n.101), kind=kOutput, calls=%fused_computation.5.clone.1 | convolution fusion | flops 810024960 | bytes 13631572 | tf_op jit(solution)/shard_map/while/body/pil,pik->lpk/dot_general | solution.py:49
  224.6 14.9 %scatter_fusion.1 = f32[768,16,128]{2,0,1:T(8,128)} fusion(f32[768,16,128]{2,0,1:T(8,128)} %get-tuple-element.265, s32[16]{0:T(128)S(1)} %get-tuple-element.247, f32[16,768,128]{2,1,0:T(8,128)} %copy.17), kind=kCustom, calls=%fused_computation.3.clone.clone.1 | custom fusion | flops 1572864 | bytes 18874432 | tf_op jit(solution)/shard_map/while/body/scatter-add | solution.py:53
  249.6 18.0 %scatter_fusion = f32[8,256,512]{2,1,0:T(8,128)} fusion(f32[8,256,512]{2,1,0:T(8,128)} %get-tuple-element.264, s32[16]{0:T(128)S(1)} %get-tuple-element.244, f32[16,256,512]{2,1,0:T(8,128)} %broadcast_multiply_fusion.2), kind=kCustom, calls=%fused_computation.2.clone.clone.1 | custom fusion | flops 2097152 | bytes 25165888 | tf_op jit(solution)/shard_map/while/body/scatter-add | solution.py:52
  271.9 7.2 %multiply_bitcast_fusion.2 = f32[16,768,128]{1,2,0:T(8,128)} fusion(f32[16]{0:T(128)S(1)} %get-tuple-element.245, bf16[16,256,768]{2,1,0:T(8,128)(2,1)} %gather_fusion.1, pred[16]{0:T(512)(128)(4,1)S(1)} %get-tuple-element.249, bf16[96,256,128]{2,1,0:T(8,128)(2,1)} %get-tuple-element.281, s32[]{:T(128)S(6)} %select_n.101), kind=kOutput, calls=%fused_computation.5.clone.1 | convolution fusion | flops 810024960 | bytes 13631572 | tf_op jit(solution)/shard_map/while/body/pil,pik->lpk/dot_general | solution.py:49
  285.6 15.1 %scatter_fusion.1 = f32[768,16,128]{2,0,1:T(8,128)} fusion(f32[768,16,128]{2,0,1:T(8,128)} %get-tuple-element.265, s32[16]{0:T(128)S(1)} %get-tuple-element.247, f32[16,768,128]{2,1,0:T(8,128)} %copy.17), kind=kCustom, calls=%fused_computation.3.clone.clone.1 | custom fusion | flops 1572864 | bytes 18874432 | tf_op jit(solution)/shard_map/while/body/scatter-add | solution.py:53
  310.8 17.6 %scatter_fusion = f32[8,256,512]{2,1,0:T(8,128)} fusion(f32[8,256,512]{2,1,0:T(8,128)} %get-tuple-element.264, s32[16]{0:T(128)S(1)} %get-tuple-element.244, f32[16,256,512]{2,1,0:T(8,128)} %broadcast_multiply_fusion.2), kind=kCustom, calls=%fused_computation.2.clone.clone.1 | custom fusion | flops 2097152 | bytes 25165888 | tf_op jit(solution)/shard_map/while/body/scatter-add | solution.py:52
  332.7 7.2 %multiply_bitcast_fusion.2 = f32[16,768,128]{1,2,0:T(8,128)} fusion(f32[16]{0:T(128)S(1)} %get-tuple-element.245, bf16[16,256,768]{2,1,0:T(8,128)(2,1)} %gather_fusion.1, pred[16]{0:T(512)(128)(4,1)S(1)} %get-tuple-element.249, bf16[96,256,128]{2,1,0:T(8,128)(2,1)} %get-tuple-element.281, s32[]{:T(128)S(6)} %select_n.101), kind=kOutput, calls=%fused_computation.5.clone.1 | convolution fusion | flops 810024960 | bytes 13631572 | tf_op jit(solution)/shard_map/while/body/pil,pik->lpk/dot_general | solution.py:49
  346.4 15.1 %scatter_fusion.1 = f32[768,16,128]{2,0,1:T(8,128)} fusion(f32[768,16,128]{2,0,1:T(8,128)} %get-tuple-element.265, s32[16]{0:T(128)S(1)} %get-tuple-element.247, f32[16,768,128]{2,1,0:T(8,128)} %copy.17), kind=kCustom, calls=%fused_computation.3.clone.clone.1 | custom fusion | flops 1572864 | bytes 18874432 | tf_op jit(solution)/shard_map/while/body/scatter-add | solution.py:53
  371.7 18.0 %scatter_fusion = f32[8,256,512]{2,1,0:T(8,128)} fusion(f32[8,256,512]{2,1,0:T(8,128)} %get-tuple-element.264, s32[16]{0:T(128)S(1)} %get-tuple-element.244, f32[16,256,512]{2,1,0:T(8,128)} %broadcast_multiply_fusion.2), kind=kCustom, calls=%fused_computation.2.clone.clone.1 | custom fusion | flops 2097152 | bytes 25165888 | tf_op jit(solution)/shard_map/while/body/scatter-add | solution.py:52
  389.7 112.0 %reduce-scatter.4.cloned.1.call-done = f32[512,512]{1,0:T(8,128)} async-done(((f32[2048,512]{1,0:T(8,128)}), f32[512,512]{1,0:T(8,128)}) %reduce-scatter.4.cloned.1.call-update) | async-done | bytes 1048592 | tf_op jit(solution)/shard_map/reduce_scatter | solution.py:64
  501.8 29.9 %reduce-scatter.6.cloned.1.call-done = f32[128,512]{1,0:T(8,128)} async-done(((f32[512,512]{1,0:T(8,128)}), f32[128,512]{1,0:T(8,128)}) %reduce-scatter.6.cloned.1.call-update) | async-done | bytes 262160 | tf_op jit(solution)/shard_map/reduce_scatter | solution.py:65
  541.2 13.3 %all-reduce.3.cloned.1.call-done = f32[768,512]{1,0:T(8,128)} async-done(((f32[768,512]{1,0:T(8,128)}), f32[768,512]{1,0:T(8,128)}) %all-reduce.3.cloned.1.call-update) | async-done | bytes 1572880 | tf_op jit(solution)/shard_map/psum | solution.py:12
  554.6 17.5 %reduce-scatter.8.cloned.1.call-done = f32[384,2048]{1,0:T(8,128)} async-done(((f32[768,2048]{1,0:T(8,128)}), f32[384,2048]{1,0:T(8,128)}) %reduce-scatter.8.cloned.1.call-update) | async-done | bytes 3145744 | tf_op jit(solution)/shard_map/reduce_scatter | solution.py:66
  576.1 119.5 %all-reduce.5.cloned.1.call-done = f32[768,512]{1,0:T(8,128)} async-done(((f32[768,512]{1,0:T(8,128)}), f32[768,512]{1,0:T(8,128)}) %all-reduce.5.cloned.1.call-update) | async-done | bytes 1572880 | tf_op jit(solution)/shard_map/psum | solution.py:12
  (61 shorter events, 116.9 us)
Async XLA Ops:
  7.2 67.8 %all-gather.2.cloned.1.call-start = ((), (), s32[]{:S(2)}) async-start(), calls=%async_computation.3 | async-start | bytes 3932160 | tf_op jit(solution)/shard_map/all_gather | solution.py:27
  7.9 493.9 %reduce-scatter.4.cloned.1.call-start = ((), (), s32[]{:S(2)}) async-start(), calls=%async_computation.4 | async-start | bytes 5242880 | tf_op jit(solution)/shard_map/reduce_scatter | solution.py:64
  78.1 5.9 copy-start.1
  389.7 142.1 %reduce-scatter.6.cloned.1.call-start = ((), (), s32[]{:S(2)}) async-start(), calls=%async_computation.5 | async-start | bytes 1310720 | tf_op jit(solution)/shard_map/reduce_scatter | solution.py:65
  501.8 52.8 %all-reduce.3.cloned.1.call-start = ((), (), s32[]{:S(2)}) async-start(), calls=%async_computation.7 | async-start | bytes 3145728 | tf_op jit(solution)/shard_map/psum | solution.py:12
  534.7 37.3 %reduce-scatter.8.cloned.1.call-start = ((), (), s32[]{:S(2)}) async-start(), calls=%async_computation.6 | async-start | bytes 9437184 | tf_op jit(solution)/shard_map/reduce_scatter | solution.py:66
  541.2 30.9 %copy-start = (f32[384,2048]{1,0:T(8,128)S(1)}, f32[384,2048]{1,0:T(8,128)}, u32[]{:S(2)}) copy-start(f32[384,2048]{1,0:T(8,128)} %param.13) | copy-start | bytes 9437188
  541.2 154.4 %all-reduce.5.cloned.1.call-start = ((), (), s32[]{:S(2)}) async-start(), calls=%async_computation.8 | async-start | bytes 3145728 | tf_op jit(solution)/shard_map/psum | solution.py:12
Sparse Core Ops, SparseCore 0:
  9.5 65.3 all-gather.1
  389.8 111.9 reduce-scatter.3
  504.6 27.0 reduce-scatter.5
  534.9 19.6 all-reduce.2
  556.7 15.3 reduce-scatter.7
  577.3 118.2 all-reduce.4
